TPU v7x, 128 devices: a whole 4x4x4 slice. The times are simulated.
128 devices in a mesh: dp: 4 (over z_hi, core), ctx: 32 (over y, z_lo, x).
Axes of the slice: x: 4, y: 4, z: 4 (z_hi: 2, z_lo: 2; z = z_hi * 2 + z_lo), core: 2. Of those that a mesh axis runs over, the one named last changes fastest.
Arguments:
- feats: bfloat16 [4, 3, 4096, 4096], P('dp', None, 'ctx'), may hold values from -6 to 6
- grad_y: bfloat16 [4, 4096, 4096], P('dp', 'ctx'), may hold values from -6 to 6
- short_w: float32 [7, 3, 4096], replicated, may hold values from -2 to 2
- long_h: float32 [4096, 4096], P(None, 'ctx'), may hold values from -2 to 2
- block_order: int32 [64], replicated, may hold values from 0 to 63, as said below
Outputs:
- mixed: bfloat16 [4, 4096, 4096], P('dp', 'ctx')
- feats_grad: bfloat16 [4, 3, 4096, 4096], P('dp', None, 'ctx')
- short_grad: float32 [7, 3, 4096], P(None, None, 'ctx')
- filter_grad: float32 [4096, 4096], P(None, 'ctx')
Inputs may be any that keep to these rules, and one draw needn't show every extreme that they name: Stored blocks 2 i and 2 i + 1 (those of index i of ctx) hold sequence blocks i and 63 - i, in an order drawn for each i; block_order is a permutation.
All inputs are finite; a program needn't handle non-finite values.
Results may differ from a plain program's by a relative error of at most 0.0085.
Values may be sent and summed in bfloat16 or wider, within the bound.
A program may use at most 192 MiB of HBM per device.

v0:
```python
import jax
import jax.numpy as jnp
import numpy as np
from jax import lax
from jax.experimental import pallas as pl
from jax.experimental.pallas import tpu as pltpu
from jax.sharding import PartitionSpec as P

MESH = pl.DeviceIdType.MESH
F32 = jnp.float32
BF16 = jnp.bfloat16
LANES = 128
TAPS = 7
ROWS = 64
WIDE = 72
OUTER = 32
GROUPS = 16
ORDER = tuple(range(OUTER // 2)) + tuple(range(OUTER - 1, OUTER // 2 - 1, -1))


def dft_tables():
    k1 = np.arange(OUTER)[:, None, None, None] + 0.5
    r = np.array(ORDER)[None, None, :, None]
    n_out = np.arange(8)[None, :, None, None]
    n_in = np.arange(8)[None, None, None, :]
    angle = 2.0 * np.pi * (r * k1 / 64.0 + n_in * k1 / 8192.0)
    keep = (n_out == n_in).astype(np.float64)
    outer = np.stack([np.cos(angle) * keep, -np.sin(angle) * keep], 1).reshape(OUTER * 16, OUTER * 8)
    n2 = np.arange(LANES)
    turn = 2.0 * np.pi * ((n2[:, None] * n2[None, :]) % LANES) / LANES
    inner = np.block([[np.cos(turn), np.sin(turn)], [-np.sin(turn), np.cos(turn)]])
    group = 2.0 * np.pi * np.arange(GROUPS)[:, None] * 8.0 * (np.arange(OUTER)[None, :] + 0.5) / 8192.0
    half = lambda a: np.asarray(np.asarray(a, np.float32), BF16)
    flat = lambda a: np.asarray(a, np.float32).reshape(-1)
    return (half(outer), half(outer.T / 4096.0), half(inner), half(inner.T), flat(np.cos(group)), flat(np.sin(group)))


def turn(i):
    a, b, c = i % 4, i // 4 % 4, i // 16
    return 8 * ((10 - a - b) % 4) + 4 * ((a + b + c + 1) % 2) + (6 - a) % 4


STEPS = [turn(i) for i in range(32) if turn(i)]


def ctx_peer(me, k):
    y, z, x = me // 8 + k // 8, me // 4 + k // 4, me + k
    return (lax.rem(y, 4) * 2 + lax.rem(z, 2)) * 4 + lax.rem(x, 4)


def ctx_source(me, k):
    y, z, x = me // 8 + 4 - k // 8, me // 4 + k // 4, me + 4 - lax.rem(k, 4)
    return (lax.rem(y, 4) * 2 + lax.rem(z, 2)) * 4 + lax.rem(x, 4)


def remote(src, dst, ssem, rsem, device):
    return pltpu.make_async_remote_copy(
        src_ref=src, dst_ref=dst, send_sem=ssem, recv_sem=rsem, device_id=device, device_id_type=MESH
    )


def wide_rows(h):
    return pl.ds(pl.multiple_of(h * 16, 16), 16)


def place(p):
    return (p, 0) if p < OUTER else (2 * OUTER - 1 - p, 1)


def scalars(cos_ref, sin_ref, h, k):
    first, second = 2 * h * OUTER + k, (2 * h + 1) * OUTER + k
    return cos_ref[first], sin_ref[first], cos_ref[second], sin_ref[second]


def outer_step(cos_ref, sin_ref, outer, pieces, mid, h):
    data = jnp.concatenate(
        [jnp.concatenate([v[:8] for v in pieces], 0), jnp.concatenate([v[8:] for v in pieces], 0)], 1
    ).astype(BF16)
    out = jnp.dot(outer[...], data, preferred_element_type=F32)
    for k in range(OUTER):
        c0, s0, c1, s1 = scalars(cos_ref, sin_ref, h, k)
        re, im = out[16 * k : 16 * k + 8], out[16 * k + 8 : 16 * k + 16]
        re0, re1, im0, im1 = re[:, :LANES], re[:, LANES:], im[:, :LANES], im[:, LANES:]
        mid[2 * k, wide_rows(h), :] = jnp.concatenate([re0 * c0 + im0 * s0, re1 * c1 + im1 * s1], 0).astype(BF16)
        mid[2 * k + 1, wide_rows(h), :] = jnp.concatenate([im0 * c0 - re0 * s0, im1 * c1 - re1 * s1], 0).astype(BF16)


def inner_forward(inner, mid, m):
    rows = [mid[pl.ds(4 * m + 2 * i, 2)].reshape(2 * LANES, LANES) for i in range(2)]
    return jnp.dot(inner[...], jnp.concatenate(rows, 1), preferred_element_type=F32)


def inner_inverse(cos_ref, sin_ref, inner_t, re, im, m, turned):
    prod = jnp.concatenate([re.astype(BF16), im.astype(BF16)], 0)
    back = jnp.dot(inner_t[...], prod, preferred_element_type=F32)
    for i in range(2):
        lanes = slice(i * LANES, (i + 1) * LANES)
        k = 2 * m + i
        for h in range(GROUPS // 2):
            c0, s0, c1, s1 = scalars(cos_ref, sin_ref, h, k)
            re0, re1 = back[16 * h : 16 * h + 8, lanes], back[16 * h + 8 : 16 * h + 16, lanes]
            im0, im1 = (back[LANES + 16 * h + o : LANES + 16 * h + o + 8, lanes] for o in (0, 8))
            rows = slice(16 * h, 16 * h + 16)
            turned[2 * k, rows, :] = jnp.concatenate([re0 * c0 - im0 * s0, re1 * c1 - im1 * s1], 0).astype(BF16)
            turned[2 * k + 1, rows, :] = jnp.concatenate([im0 * c0 + re0 * s0, im1 * c1 + re1 * s1], 0).astype(BF16)


def outer_inverse(outer_t, turned, h):
    values = turned[:, wide_rows(h), :].astype(F32)
    sides = [values[:, o : o + 8].reshape(OUTER * 16, LANES) for o in (0, 8)]
    out = jnp.dot(outer_t[...], jnp.concatenate(sides, 1).astype(BF16), preferred_element_type=F32)
    pieces = []
    for i in range(OUTER):
        part = out[8 * i : 8 * i + 8]
        pieces.append(jnp.concatenate([part[:, :LANES], part[:, LANES:]], 0))
    return pieces


def both_halves(step):
    for odd in range(2):

        def body(i, carry, odd=odd):
            step(4 * odd + i, odd, wide_rows(i))
            return carry

        lax.fori_loop(0, 4, body, 0, unroll=2)


def hyena_kernel(
    cos_ref, sin_ref, order_ref, outer, outer_t, inner, inner_t, long_h, w_ref, x_hbm, g_hbm,
    mixed_ref, grad_ref, filt, total,
    send, recv, mid, spec_h, spec_g, spec_c, turned, cross, out, local, pair, near, far,
    back, qkv_ref, x_ref, g_ref, shifted, part, held, dp_held,
    tail, head, got_tail, got_head,
    send_in, recv_in, send_out, recv_out, own_sem, dp_send, dp_recv,
    load_sem, part_send, part_recv, sum_send, sum_recv, halo_send, halo_recv,
):
    n = send.shape[1]
    me = lax.axis_index("ctx")
    mine = lax.axis_index("dp")
    core = lax.rem(mine, 2)
    neighbour = {"dp": mine + 1 - 2 * core}
    opposite = {"dp": lax.rem(mine + 2, 4)}
    barrier = pltpu.get_barrier_semaphore()
    for k in STEPS:
        pl.semaphore_signal(barrier, inc=1, device_id={"ctx": ctx_peer(me, k)}, device_id_type=MESH)
    diagonal = {"dp": lax.rem(mine + 3 - 2 * core, 4)}
    for device in (neighbour, opposite, diagonal):
        pl.semaphore_signal(barrier, inc=1, device_id=device, device_id_type=MESH)
    loads = [
        pltpu.make_async_copy(source, target, load_sem.at[i])
        for i, (source, target) in enumerate(((x_hbm, x_ref), (g_hbm, g_ref)))
    ]
    for copy in loads:
        copy.start()
    flip = (order_ref[2 * me] != me).astype(jnp.int32)
    for copy in loads:
        copy.wait()
    for way, (ends, starts) in enumerate(((flip, 1 - flip), (1 - flip, flip))):
        for j in range(3):
            tail[way, j] = x_ref[j, ends, ROWS - 8 :, :]
            head[way, j] = x_ref[j + 1, starts, :8, :] if j < 2 else g_ref[starts, :8, :]
    pl.semaphore_wait(barrier, n + 2)
    aside = ({"ctx": lax.rem(me + 1, n)}, {"ctx": lax.rem(me + n - 1, n)})
    halos = [
        remote(source.at[way], target.at[way], halo_send.at[i, way], halo_recv.at[i, way], aside[way])
        for i, (source, target) in enumerate(((tail, got_tail), (head, got_head)))
        for way in range(2)
    ]
    for copy in halos:
        copy.start()

    def inward(a, k):
        peer = ctx_peer(me, k)
        return remote(send.at[a, peer], recv.at[a, me], send_in.at[a, k], recv_in.at[a, k], {"ctx": peer})

    def outward(a, k):
        peer = ctx_peer(me, k)
        return remote(out.at[a, peer], back.at[a, me], send_out.at[a, k], recv_out.at[a, k], {"ctx": peer})

    def filter_outer(h, odd, row):
        del odd, row
        pieces = [long_h[pl.ds(pl.multiple_of(r * LANES + h * 16, 16), 16), :] for r in ORDER]
        outer_step(cos_ref, sin_ref, outer, pieces, mid, h)

    both_halves(filter_outer)

    def filter_inner(m, carry):
        spec_h[m] = inner_forward(inner, mid, m)
        return carry

    lax.fori_loop(0, OUTER // 2, filter_inner, 0, unroll=2)

    for copy in halos[:2]:
        copy.wait_recv()
    first, last = me == 0, me == n - 1

    def lanes_of(owner):
        return pl.ds(pl.multiple_of(owner * LANES, LANES), LANES)

    def featurize(owner):
        lanes = lanes_of(owner)
        for half in range(2):
            stored = 1 - flip if half else flip
            values = []
            for j in range(3):
                came = got_tail[half, j, :, lanes].astype(F32)
                if half == 0:
                    before = jnp.where(first, jnp.zeros_like(came), came)
                else:
                    before = jnp.where(last, tail[0, j, :, lanes].astype(F32), came)
                shifted[half, j, :8] = before
                shifted[half, j, 8:] = x_ref[j, stored, :, lanes].astype(F32)
                acc = None
                for t in range(TAPS):
                    term = w_ref[j, t : t + 1, lanes] * shifted[half, j, pl.ds(8 - t, ROWS), :]
                    acc = term if acc is None else acc + term
                value = acc.astype(BF16)
                qkv_ref[j, half, :, lanes] = value
                values.append(value.astype(F32))
            send[0, owner, half] = (values[1] * values[2]).astype(BF16)
            send[1, owner, half] = (g_ref[stored, :, lanes].astype(F32) * values[0]).astype(BF16)

    def start_gated(i):
        k = turn(i)

        @pl.when(k > 0)
        def _():
            inward(0, k).start()

    featurize(ctx_peer(me, turn(0)))

    def featurize_next(i, carry):
        featurize(ctx_peer(me, turn(i)))
        start_gated(i - 1)
        return carry

    lax.fori_loop(1, n, featurize_next, 0)
    start_gated(n - 1)
    own_in = [pltpu.make_async_copy(send.at[a, me], recv.at[a, me], own_sem.at[a]) for a in range(2)]
    for copy in own_in:
        copy.start()
    for k in STEPS:
        inward(1, k).start()

    def arrive(a):
        own_in[a].wait()
        for k in STEPS:
            inward(a, k).wait_recv()

        def step(h, odd, row):
            places = [place(2 * r + odd) for r in ORDER]
            pieces = [recv[a, owner, half, row, :].astype(F32) for owner, half in places]
            outer_step(cos_ref, sin_ref, outer, pieces, mid, h)

        both_halves(step)

    def depart(a, turned):
        def step(h, odd, row):
            for r, piece in zip(ORDER, outer_inverse(outer_t, turned, h)):
                owner, half = place(2 * r + odd)
                out[a, owner, half, row, :] = piece.astype(BF16)

        both_halves(step)
        for p in range(2 * n):
            owner, half = place(p)
            if p + 1 < 2 * n:
                after, part = place(p + 1)
                out[a, owner, half, ROWS:, :] = out[a, after, part, : WIDE - ROWS, :]
            else:
                out[a, owner, half, ROWS:, :] = jnp.zeros((WIDE - ROWS, LANES), BF16)
        for k in STEPS:
            outward(a, k).start()
        own = pltpu.make_async_copy(out.at[a, me], back.at[a, me], own_sem.at[2 + a])
        own.start()
        return own

    arrive(0)

    def conv_step(m, carry):
        g = inner_forward(inner, mid, m)
        spec_g[m] = g
        h = spec_h[m]
        gr, gi, hr, hi = g[:LANES], g[LANES:], h[:LANES], h[LANES:]
        inner_inverse(cos_ref, sin_ref, inner_t, gr * hr - gi * hi, gr * hi + gi * hr, m, turned)
        return carry

    lax.fori_loop(0, OUTER // 2, conv_step, 0, unroll=2)
    own_conv = depart(0, turned)

    arrive(1)

    def grad_step(m, carry):
        c = inner_forward(inner, mid, m)
        spec_c[m] = c
        h = spec_h[m]
        cr, ci, hr, hi = c[:LANES], c[LANES:], h[:LANES], h[LANES:]
        inner_inverse(cos_ref, sin_ref, inner_t, cr * hr + ci * hi, ci * hr - cr * hi, m, turned)
        return carry

    lax.fori_loop(0, OUTER // 2, grad_step, 0, unroll=2)

    def cross_step(m, carry):
        c, g = spec_c[m], spec_g[m]
        cr, ci, gr, gi = c[:LANES], c[LANES:], g[:LANES], g[LANES:]
        inner_inverse(cos_ref, sin_ref, inner_t, cr * gr + ci * gi, ci * gr - cr * gi, m, cross)
        return carry

    lax.fori_loop(0, OUTER // 2, cross_step, 0, unroll=2)

    def filter_back(h, odd, row):
        del odd, row
        for r, piece in zip(ORDER, outer_inverse(outer_t, cross, h)):
            local[r, wide_rows(h), :] = piece

    both_halves(filter_back)

    half = OUTER // 2
    kept = pl.ds(core * half, half)
    given = pl.ds((1 - core) * half, half)
    to_pair = remote(local.at[given], pair, dp_send.at[0], dp_recv.at[0], neighbour)
    to_pair.start()
    own_grad = depart(1, turned)

    def add_far(i, carry):
        filt[core * half + i] = near[i].astype(F32) + far[i].astype(F32)
        return carry

    for copy in halos[2:]:
        copy.wait_recv()

    def taps_back(j, half, inside, beyond, source, sums):
        shifted[half, j, :ROWS] = inside
        shifted[half, j, ROWS:] = beyond
        acc = None
        for t in range(TAPS):
            value = shifted[half, j, pl.ds(t, ROWS), :]
            term = w_ref[j, t : t + 1, sums[0]] * value
            acc = term if acc is None else acc + term
            fold = jnp.sum((source * value).reshape(8, 8, LANES), axis=0)
            sums[1][j][t] = fold if half == 0 else sums[1][j][t] + fold
        return acc

    def put_part(owner, j, folds):
        rows = [jnp.sum(value, axis=0, keepdims=True) for value in folds]
        part[owner, 8 * j : 8 * j + 8, :] = jnp.concatenate([*rows, jnp.zeros((1, LANES), F32)], 0)

    def in_order(values):
        keep = flip == 0
        return [jnp.where(keep, values[i], values[1 - i]).astype(BF16) for i in range(2)]

    def after_rows(half, rim, lanes):
        came = got_head[1 - half, rim, :, lanes].astype(F32)
        if half == 0:
            return jnp.where(last, head[0, rim, :, lanes].astype(F32), came)
        return jnp.where(first, jnp.zeros_like(came), came)

    def finish_query(owner):
        lanes = lanes_of(owner)
        mixed, grads, folds = [], [], [[None] * TAPS]
        for half in range(2):
            stored = 1 - flip if half else flip
            conv = back[0, owner, half].astype(F32)
            mixed.append(qkv_ref[0, half, :, lanes].astype(F32) * conv[:ROWS])
            inside = (g_ref[stored, :, lanes].astype(F32) * conv[:ROWS]).astype(BF16).astype(F32)
            beyond = (after_rows(half, 2, lanes) * conv[ROWS:]).astype(BF16).astype(F32)
            source = x_ref[0, stored, :, lanes].astype(F32)
            grads.append(taps_back(0, half, inside, beyond, source, (lanes, folds)))
        for i, (value, grad) in enumerate(zip(in_order(mixed), in_order(grads))):
            mixed_ref[i, :, lanes] = value
            grad_ref[0, i, :, lanes] = grad
        put_part(owner, 0, folds[0])

    def finish_gate(owner):
        lanes = lanes_of(owner)
        grads, folds = [[], [], []], [[None] * TAPS for _ in range(3)]
        for half in range(2):
            stored = 1 - flip if half else flip
            gate_grad = back[1, owner, half].astype(F32)
            sources = {j: x_ref[j, stored, :, lanes].astype(F32) for j in (1, 2)}
            for j in (1, 2):
                other = 3 - j
                ext = jnp.concatenate([sources[other][ROWS - 8 :], after_rows(half, other - 1, lanes)], 0)
                more = w_ref[other, 0:1, lanes] * ext[8:]
                for t in range(1, TAPS):
                    more = more + w_ref[other, t : t + 1, lanes] * ext[8 - t : 16 - t]
                inside = gate_grad[:ROWS] * qkv_ref[other, half, :, lanes].astype(F32)
                beyond = gate_grad[ROWS:] * more.astype(BF16).astype(F32)
                grads[j].append(taps_back(j, half, inside, beyond, sources[j], (lanes, folds)))
        for j in (1, 2):
            for i, grad in enumerate(in_order(grads[j])):
                grad_ref[j, i, :, lanes] = grad
            put_part(owner, j, folds[j])

    def part_back(k):
        owner = ctx_source(me, k)
        return remote(part.at[owner], held.at[me], part_send.at[k], part_recv.at[k], {"ctx": owner})

    own_conv.wait()

    def query_next(i, carry):
        k = turn(i)

        @pl.when(k > 0)
        def _():
            outward(0, k).wait_recv()

        finish_query(ctx_source(me, k))
        return carry

    lax.fori_loop(0, n, query_next, 0)
    to_pair.wait()

    def add_pair(i, carry):
        near[i] = (local[core * half + i] + pair[i]).astype(BF16)
        return carry

    lax.fori_loop(0, half, add_pair, 0)
    across = remote(near, far, dp_send.at[1], dp_recv.at[1], opposite)
    across.start()
    own_grad.wait()

    def start_part(i):
        k = turn(i)

        @pl.when(k > 0)
        def _():
            part_back(k).start()

    def gate_next(i, carry):
        k = turn(i)

        @pl.when(k > 0)
        def _():
            outward(1, k).wait_recv()

        finish_gate(ctx_source(me, k))

        @pl.when(i > 0)
        def _():
            start_part(i - 1)

        return carry

    lax.fori_loop(0, n, gate_next, 0)
    start_part(n - 1)
    held[me] = part[me]
    across.wait()
    lax.fori_loop(0, half, add_far, 0)
    to_whole = remote(filt.at[kept], filt.at[kept], dp_send.at[2], dp_recv.at[2], neighbour)
    to_whole.start()
    for k in STEPS:
        part_back(k).wait_recv()
    dp_held[mine] = jnp.sum(held[...], axis=0)
    sums_out = [
        remote(dp_held.at[mine], dp_held.at[mine], sum_send.at[i], sum_recv.at[i], {"dp": lax.rem(mine + i, 4)})
        for i in range(1, 4)
    ]
    for copy in sums_out:
        copy.start()
    for copy in sums_out:
        copy.wait()
    sums = (dp_held[0] + dp_held[1]) + (dp_held[2] + dp_held[3])
    for j in range(3):
        total[j] = sums[8 * j : 8 * j + TAPS]
    to_whole.wait()
    for copy in halos:
        copy.wait_send()
    for k in STEPS:
        part_back(k).wait_send()
        for a in range(2):
            inward(a, k).wait_send()
            outward(a, k).wait_send()


def hyena(order, long_h, w, x, g):
    outer, outer_t, inner, inner_t, cos_g, sin_g = dft_tables()
    width = x.shape[-1]
    n = width // LANES
    vmem, smem, hbm = (pl.BlockSpec(memory_space=m) for m in (pltpu.VMEM, pltpu.SMEM, pl.ANY))
    cube, sums = (OUTER, LANES, LANES), (24, LANES)
    dma = pltpu.SemaphoreType.DMA
    mixed_shape, grad_shape = (2, ROWS, width), (3, 2, ROWS, width)
    token_blocks, back_blocks = (2, n, 2, ROWS, LANES), (2, n, 2, WIDE, LANES)
    half_cube = (OUTER // 2, LANES, LANES)
    spectrum = (OUTER // 2, 2 * LANES, 2 * LANES)
    stage = (2 * OUTER, LANES, LANES)
    return pl.pallas_call(
        hyena_kernel,
        out_shape=[
            pltpu.VMEM(mixed_shape, BF16),
            pltpu.VMEM(grad_shape, BF16),
            pltpu.VMEM(cube, F32),
            jax.ShapeDtypeStruct((3, TAPS, LANES), F32),
        ],
        in_specs=[smem] * 3 + [vmem] * 6 + [hbm] * 2,
        out_specs=[vmem] * 4,
        scratch_shapes=[
            *[pltpu.VMEM(token_blocks, BF16)] * 2,
            pltpu.VMEM(stage, BF16),
            *[pltpu.VMEM(spectrum, F32)] * 3,
            *[pltpu.VMEM(stage, BF16)] * 2,
            pltpu.VMEM(back_blocks, BF16),
            pltpu.VMEM(cube, F32),
            pltpu.VMEM(half_cube, F32),
            *[pltpu.VMEM(half_cube, BF16)] * 2,
            pltpu.VMEM(back_blocks, BF16),
            *[pltpu.VMEM(grad_shape, BF16)] * 2,
            pltpu.VMEM(mixed_shape, BF16),
            pltpu.VMEM((2, 3, ROWS + 8, LANES), F32),
            *[pltpu.VMEM((n, *sums), F32)] * 2,
            pltpu.VMEM((4, *sums), F32),
            *[pltpu.VMEM((2, 3, 8, width), BF16)] * 4,
            *[dma((2, n))] * 4,
            dma((4,)),
            dma((3,)),
            dma((3,)),
            dma((2,)),
            *[dma((n,))] * 2,
            *[dma((4,))] * 2,
            *[dma((2, 2))] * 2,
        ],
        compiler_params=pltpu.CompilerParams(collective_id=1, has_side_effects=True, vmem_limit_bytes=48 << 20),
        name="hyena",
    )(cos_g, sin_g, order, outer, outer_t, inner, inner_t, long_h, w, x, g)


def on_device(feats, grad_y, short_w, long_h, block_order):
    width = feats.shape[3]
    x = feats.reshape(3, 2, ROWS, width)
    g = grad_y.reshape(2, ROWS, width)
    mixed, grads, filt, short = hyena(block_order, long_h, jnp.transpose(short_w, (1, 0, 2)), x, g)
    return (
        mixed.reshape(grad_y.shape),
        grads.reshape(feats.shape),
        jnp.transpose(short, (1, 0, 2)),
        filt.reshape(OUTER * LANES, LANES),
    )


def solution(mesh):
    placed = (P("dp", None, "ctx", None), P("dp", "ctx", None), P(), P(None, "ctx"), P())
    return jax.shard_map(
        on_device,
        mesh=mesh,
        in_specs=placed,
        out_specs=(P("dp", "ctx", None), P("dp", None, "ctx", None), P(None, None, "ctx"), P(None, "ctx")),
        check_vma=False,
    )
```

profile of v0, /device:TPU:1, one launch (start us, length us, event | category | flops | bytes accessed | tf_op | source)
XLA Modules:
  0.0 100.0 jit_solution(6647922366351059909)
XLA Ops:
  0.6 94.8 %hyena.1 = (bf16[2,64,4096]{2,1,0:T(8,128)(2,1)S(1)}, bf16[3,2,64,4096]{3,2,1,0:T(8,128)(2,1)S(1)}, f32[32,128,128]{2,1,0:T(8,128)S(1)}, f32[3,7,128]{2,1,0:T(8,128)}) custom-call(f32[512]{0:T(512)} %constant.12.clone.cos_ref, f32[512]{0:T(512)} %constant.13.clone.sin_ref, s32[64]{0:T(128)} %order_ref.1, bf16[512,256]{1,0:T(8,128)(2,1)} %constant.14.clone.outer, ...), custom_call_target="tpu_custom_call" | custom-call | tf_op jit(solution)/shard_map/hyena/pallas_call | solution.py:488
  95.4 1.0 copy.19
  96.4 1.7 %copy.20 = bf16[1,3,128,4096]{3,2,1,0:T(8,128)(2,1)} copy(bf16[1,3,128,4096]{3,2,1,0:T(8,128)(2,1)S(1)} %bitcast.7) | data formatting | bytes 6291456
  98.0 0.0 copy-start
  98.0 1.3 %copy.21 = f32[4096,128]{1,0:T(8,128)} copy(f32[4096,128]{1,0:T(8,128)S(1)} %bitcast.8) | data formatting | bytes 4194304
  99.4 0.0 copy-done
  99.4 0.6 copy.22
Async XLA Ops:
  98.0 1.3 %copy-start = (f32[3,7,128]{2,1,0:T(8,128)S(1)}, f32[3,7,128]{2,1,0:T(8,128)}, u32[]{:S(2)}) copy-start(f32[3,7,128]{2,1,0:T(8,128)} %get-tuple-element.10) | copy-start | bytes 32260
where the time goes:
time: 100 us
  Pallas kernels  94.8 us (95%)
  local copies, waits for them, and re-layouts  4.56 us (5%)
    pallas_call x1, Pallas kernels, hyena(): pl.pallas_call(hyena_kernel, out_shape=[pltpu.VMEM(mixed_shape, BF16), pl...  94.8 us
    unnamed x6, local copies, waits for them, and re-layouts  4.56 us

commit v1 on v0

--- a/solution.py
+++ b/solution.py
@@ -445,10 +445,6 @@
     lax.fori_loop(0, n, gate_next, 0)
     start_part(n - 1)
     held[me] = part[me]
-    across.wait()
-    lax.fori_loop(0, half, add_far, 0)
-    to_whole = remote(filt.at[kept], filt.at[kept], dp_send.at[2], dp_recv.at[2], neighbour)
-    to_whole.start()
     for k in STEPS:
         part_back(k).wait_recv()
     dp_held[mine] = jnp.sum(held[...], axis=0)
@@ -458,6 +454,10 @@
     ]
     for copy in sums_out:
         copy.start()
+    across.wait()
+    lax.fori_loop(0, half, add_far, 0)
+    to_whole = remote(filt.at[kept], filt.at[kept], dp_send.at[2], dp_recv.at[2], neighbour)
+    to_whole.start()
     for copy in sums_out:
         copy.wait()
     sums = (dp_held[0] + dp_held[1]) + (dp_held[2] + dp_held[3])

time: 100 us -> 100 us (level)
  no operation moved by 1% of the time
where the time goes in v1:
time: 100 us; the launch traced here: 99.9 us
  Pallas kernels  94.7 us (95%)
  local copies, waits for them, and re-layouts  4.56 us (5%)
    pallas_call x1, Pallas kernels, hyena(): pl.pallas_call(hyena_kernel, out_shape=[pltpu.VMEM(mixed_shape, BF16), pl...  94.7 us
    unnamed x6, local copies, waits for them, and re-layouts  4.56 us

profile of v1, /device:TPU:1, one launch (start us, length us, event | category | flops | bytes accessed | tf_op | source)
XLA Modules:
  0.0 99.9 jit_solution(18430631965099575245)
XLA Ops:
  0.6 94.7 %hyena.1 = (bf16[2,64,4096]{2,1,0:T(8,128)(2,1)S(1)}, bf16[3,2,64,4096]{3,2,1,0:T(8,128)(2,1)S(1)}, f32[32,128,128]{2,1,0:T(8,128)S(1)}, f32[3,7,128]{2,1,0:T(8,128)}) custom-call(f32[512]{0:T(512)} %constant.12.clone.cos_ref, f32[512]{0:T(512)} %constant.13.clone.sin_ref, s32[64]{0:T(128)} %order_ref.1, bf16[512,256]{1,0:T(8,128)(2,1)} %constant.14.clone.outer, ...), custom_call_target="tpu_custom_call" | custom-call | tf_op jit(solution)/shard_map/hyena/pallas_call | solution.py:488
  95.4 1.0 copy.19
  96.3 1.7 %copy.20 = bf16[1,3,128,4096]{3,2,1,0:T(8,128)(2,1)} copy(bf16[1,3,128,4096]{3,2,1,0:T(8,128)(2,1)S(1)} %bitcast.7) | data formatting | bytes 6291456
  98.0 0.0 copy-start
  98.0 1.3 %copy.21 = f32[4096,128]{1,0:T(8,128)} copy(f32[4096,128]{1,0:T(8,128)S(1)} %bitcast.8) | data formatting | bytes 4194304
  99.3 0.0 copy-done
  99.3 0.6 copy.22
Async XLA Ops:
  98.0 1.3 %copy-start = (f32[3,7,128]{2,1,0:T(8,128)S(1)}, f32[3,7,128]{2,1,0:T(8,128)}, u32[]{:S(2)}) copy-start(f32[3,7,128]{2,1,0:T(8,128)} %get-tuple-element.10) | copy-start | bytes 32260
